TPU v7x, 128 devices: a whole 4x4x4 slice. The times are simulated.
128 devices in a mesh: gx: 16 (over z_lo, x, core), gz: 8 (over y, z_hi).
Axes of the slice: x: 4, y: 4, z: 4 (z_hi: 2, z_lo: 2; z = z_hi * 2 + z_lo), core: 2. Of those that a mesh axis runs over, the one named last changes fastest.
Arguments:
- elevation: float32 [2048, 2048], P(('gx', 'gz')), may hold values from -2 to 2
- potential: float32 [2048, 2048], P(('gx', 'gz')), may hold values from -6 to 6
- tracer: float32 [2048, 64, 256], P('gx', 'gz'), may hold values from -6 to 6
- wind_speed: float32 [2048, 64, 256], P('gx', 'gz'), may hold values from -4 to 4
Outputs:
- new_elevation: float32 [2048, 2048], P(('gx', 'gz'))
- new_tracer: float32 [2048, 64, 256], P('gx', 'gz')
All inputs are finite; a program needn't handle non-finite values.
Results may differ from a plain program's by a relative error of at most 0.00019.
Values sent between devices are 32-bit elements; how exact they have to be, the bound alone decides.
No kernel may reach another device: no remote copies, remote signals or barrier semaphores. Data moves between devices by JAX's collectives and lax.ppermute only.
A program may use at most 128 MiB of HBM per device.

v0:
```python
import jax
import jax.numpy as jnp
from jax import lax
from jax.sharding import PartitionSpec as P

NS = 2048
TWO_PI = 6.283185307179586
DT_WAVE = 0.05
COLUMN_DEPTH = 32.0
DT_AIR = 0.1
NU_AIR = 0.2
PRECISE = lax.Precision.HIGHEST


def padded_2(shard, sides, width, wrap):
    for axis, dim in sides:
        size, length = (lax.axis_size(axis), shard.shape[dim])
        up = [(i, (i + 1) % size) for i in range(size if wrap else size - 1)]
        down = [(j, i) for i, j in up]
        last = lax.slice_in_dim(shard, length - width, length, axis=dim)
        leading = lax.slice_in_dim(shard, 0, width, axis=dim)
        before = lax.ppermute(last, axis, up)
        after = lax.ppermute(leading, axis, down)
        shard = jnp.concatenate([before, shard, after], axis=dim)
    return shard


def angle_table(row_count, col_count, length):
    row_index = jnp.arange(row_count, dtype=jnp.int32)
    col_index = jnp.arange(col_count, dtype=jnp.int32)
    product = row_index[:, None] * col_index[None, :] % length
    angles = product.astype(jnp.float32) * (TWO_PI / length)
    return (jnp.cos(angles), jnp.sin(angles))


def contract(pattern, real_part, imaginary, cosine, sine, sign_value, keep_imaginary):
    real_cosine = jnp.einsum(pattern, real_part, cosine, precision=PRECISE)
    real_sine = jnp.einsum(pattern, real_part, sine, precision=PRECISE)
    if imaginary is None:
        return (real_cosine, sign_value * real_sine)
    imag_sine = jnp.einsum(pattern, imaginary, sine, precision=PRECISE)
    out_real = real_cosine - sign_value * imag_sine
    if not keep_imaginary:
        return (out_real, None)
    imag_cosine = jnp.einsum(pattern, imaginary, cosine, precision=PRECISE)
    return (out_real, imag_cosine + sign_value * real_sine)


def twist_phase(real_part, imaginary, cosine, sine, sign_value):
    out_real = real_part * cosine - sign_value * imaginary * sine
    out_imag = imaginary * cosine + sign_value * real_part * sine
    return (out_real, out_imag)


def transform_last(real_part, imaginary, inverse, keep_imaginary):
    length = real_part.shape[-1]
    inner_size = 128
    outer_size = length // inner_size
    leading = real_part.shape[:-1]
    sign_value = 1.0 if inverse else -1.0
    cosine_outer, sine_outer = angle_table(outer_size, outer_size, outer_size)
    cosine_inner, sine_inner = angle_table(inner_size, inner_size, inner_size)
    cosine_twist, sine_twist = angle_table(outer_size, inner_size, length)
    real_part = real_part.reshape(leading + (outer_size, inner_size))
    if imaginary is not None:
        imaginary = imaginary.reshape(leading + (outer_size, inner_size))
    if not inverse:
        real_part, imaginary = contract(
            "...an,ak->...kn", real_part, imaginary, cosine_outer, sine_outer, sign_value, True
        )
        real_part, imaginary = twist_phase(
            real_part, imaginary, cosine_twist, sine_twist, sign_value
        )
        real_part, imaginary = contract(
            "...kn,nb->...kb", real_part, imaginary, cosine_inner, sine_inner, sign_value, True
        )
        return (real_part.reshape(leading + (length,)), imaginary.reshape(leading + (length,)))
    real_part, imaginary = contract(
        "...kb,bn->...kn", real_part, imaginary, cosine_inner, sine_inner, sign_value, True
    )
    real_part, imaginary = twist_phase(real_part, imaginary, cosine_twist, sine_twist, sign_value)
    real_part, imaginary = contract(
        "...kn,ka->...an",
        real_part,
        imaginary,
        cosine_outer,
        sine_outer,
        sign_value,
        keep_imaginary,
    )
    factor = 1.0 / length
    real_part = real_part.reshape(leading + (length,)) * factor
    if imaginary is None:
        return (real_part, None)
    return (real_part, imaginary.reshape(leading + (length,)) * factor)


def permuted_waves(positions, length):
    inner_size = 128
    outer_size = length // inner_size
    wave_index = positions // inner_size + outer_size * (positions % inner_size)
    signed = jnp.where(wave_index < length // 2, wave_index, wave_index - length).astype(
        jnp.float32
    ) * (TWO_PI / length)
    odd_wave = jnp.where(wave_index == length // 2, 0.0, signed)
    return (signed, odd_wave)


def block_start(block_rows):
    return (lax.axis_index("gx") * lax.axis_size("gz") + lax.axis_index("gz")) * block_rows


def to_columns(stacked):
    return lax.all_to_all(stacked, ("gx", "gz"), split_axis=3, concat_axis=2, tiled=True)


def to_rows(stacked):
    return lax.all_to_all(stacked, ("gx", "gz"), split_axis=2, concat_axis=3, tiled=True)


def spectra(fields):
    real_part, imaginary = transform_last(fields, None, False, True)
    stacked = jnp.stack([real_part, imaginary], 1)
    turned = jnp.swapaxes(to_columns(stacked), 2, 3)
    return transform_last(turned[:, 0], turned[:, 1], False, True)


def fields_back(real_part, imaginary):
    real_part, imaginary = transform_last(real_part, imaginary, True, True)
    stacked = jnp.swapaxes(jnp.stack([real_part, imaginary], 1), 2, 3)
    turned = to_rows(stacked)
    return transform_last(turned[:, 0], turned[:, 1], True, False)


def fields_from(spectrum_list):
    members = len(spectrum_list)
    real_part, unused = fields_back(
        jnp.stack([member[0] for member in spectrum_list]),
        jnp.stack([member[1] for member in spectrum_list]),
    )
    return [real_part[offset] for offset in range(members)]


def scaled(real_part, imaginary, factor):
    return (factor * real_part, factor * imaginary)


def derived(real_part, imaginary, factor):
    return (-factor * imaginary, factor * real_part)


def level_rims(field):
    padded = padded_2(field, (("gz", 1),), 1, False)
    bottom = lax.axis_index("gz") == 0
    top_device = lax.axis_index("gz") == lax.axis_size("gz") - 1
    lower_level = jnp.concatenate(
        [jnp.where(bottom, field[:, :1], padded[:, :1]), field[:, :-1]], 1
    )
    upper_level = jnp.concatenate(
        [field[:, 1:], jnp.where(top_device, field[:, -1:], padded[:, -1:])], 1
    )
    return (lower_level, upper_level)


def shards(elevation, potential, tracer, wind_speed):
    block_rows = elevation.shape[0]
    real_part, imaginary = spectra(jnp.stack([elevation, potential]))
    positions = block_start(block_rows) + jnp.arange(block_rows, dtype=jnp.int32)
    wave_y, odd_y = permuted_waves(positions, NS)
    wave_x, odd_x = permuted_waves(jnp.arange(NS, dtype=jnp.int32), NS)
    magnitude = jnp.sqrt(wave_x[None, :] * wave_x[None, :] + wave_y[:, None] * wave_y[:, None])
    squared = magnitude * magnitude
    magnitude_cube = squared * magnitude
    along_x = odd_x[None, :] + jnp.zeros_like(magnitude)
    along_y = odd_y[:, None] + jnp.zeros_like(magnitude)
    eta_real, eta_imag = (real_part[0], imaginary[0])
    phi_real, phi_imag = (real_part[1], imaginary[1])
    first_once, first_twice, first_thrice, slope_x, slope_y, speed_x, speed_y = fields_from(
        [
            scaled(phi_real, phi_imag, magnitude),
            scaled(phi_real, phi_imag, squared),
            scaled(phi_real, phi_imag, magnitude_cube),
            derived(eta_real, eta_imag, along_x),
            derived(eta_real, eta_imag, along_y),
            derived(phi_real, phi_imag, along_x),
            derived(phi_real, phi_imag, along_y),
        ]
    )
    second_field = -elevation * first_once
    real_part, imaginary = spectra(second_field[None])
    second_once, second_twice = fields_from(
        [scaled(real_part[0], imaginary[0], magnitude), scaled(real_part[0], imaginary[0], squared)]
    )
    third_field = -elevation * second_once - 0.5 * elevation * elevation * first_twice
    real_part, imaginary = spectra(third_field[None])
    third_list = fields_from([scaled(real_part[0], imaginary[0], magnitude)])
    third_once = third_list[0]
    vertical = (
        first_once
        + elevation * first_twice
        + 0.5 * elevation * elevation * first_thrice
        + second_once
        + elevation * second_twice
        + third_once
    )
    tendency = (
        -(slope_x * speed_x + slope_y * speed_y)
        + (1.0 + slope_x * slope_x + slope_y * slope_y) * vertical
    )
    new_elevation = elevation + DT_WAVE * tendency
    columns = tracer.shape[2]
    padded = padded_2(tracer, (("gx", 0),), 1, True)
    eastern = padded[2:]
    western = padded[:-2]
    northern = jnp.concatenate([tracer[:, :, 1:], tracer[:, :, -1:]], 2)
    southern = jnp.concatenate([tracer[:, :, :1], tracer[:, :, :-1]], 2)
    moved_tracer = tracer + DT_AIR * (
        -wind_speed * (eastern - western) * 0.5
        + NU_AIR * (eastern + western + northern + southern - 4.0 * tracer)
    )
    real_part, imaginary = spectra(new_elevation[None])
    slope_list = fields_from([derived(real_part[0], imaginary[0], along_x)])
    new_slope = slope_list[0]
    window = jnp.stack([elevation[:, :columns], new_elevation[:, :columns], new_slope[:, :columns]])
    surface = lax.all_gather(window, "gz", axis=1, tiled=True)
    old_rows = surface[0]
    new_rows = surface[1]
    slope_rows = surface[2]
    levels = tracer.shape[1]
    level_count = levels * lax.axis_size("gz")
    sigma_level = (
        (lax.axis_index("gz") * levels + jnp.arange(levels, dtype=jnp.int32)).astype(jnp.float32)
        + 0.5
    ) / level_count
    lift_factor = (1.0 - sigma_level)[None, :, None]
    level_shift = (
        ((new_rows - old_rows) / (COLUMN_DEPTH - old_rows))[:, None, :] * lift_factor * level_count
    )
    lower_level, upper_level = level_rims(moved_tracer)
    remapped = (
        moved_tracer
        + 0.5 * level_shift * (upper_level - lower_level)
        + 0.5 * level_shift * level_shift * (upper_level - 2.0 * moved_tracer + lower_level)
    )
    lower_level, upper_level = level_rims(remapped)
    column_depth = (COLUMN_DEPTH - new_rows)[:, None, :]
    advection = (
        wind_speed
        * lift_factor
        * slope_rows[:, None, :]
        / column_depth
        * (upper_level - lower_level)
        * (0.5 * level_count)
    )
    spread_term = (
        NU_AIR
        * (upper_level - 2.0 * remapped + lower_level)
        * (level_count * level_count)
        / (column_depth * column_depth)
    )
    new_tracer = remapped + DT_AIR * (advection + spread_term)
    return (new_elevation, new_tracer)


def solution(mesh):
    return jax.shard_map(
        shards,
        mesh=mesh,
        in_specs=(
            P(("gx", "gz"), None),
            P(("gx", "gz"), None),
            P("gx", "gz", None),
            P("gx", "gz", None),
        ),
        out_specs=(P(("gx", "gz"), None), P("gx", "gz", None)),
        check_vma=False,
    )
```

profile of v0, /device:TPU:8, one launch (start us, length us, event | category | flops | bytes accessed | tf_op | source)
XLA Modules:
  0.0 606.4 jit_solution(7506074649540263558)
XLA Ops:
  10.3 7.0 %fusion.923 = f32[2048,2,2,16]{3,2,1,0:T(2,128)} fusion(f32[2,1,16,2048]{2,1,0,3:T(1,128)} %bitcast.800, f32[2,1,16,2048]{2,1,0,3:T(1,128)S(1)} %bitcast.798), kind=kLoop, calls=%fused_computation.1021 | loop fusion | flops 131072 | bytes 1048576
  17.3 8.0 %reshape.1070 = f32[128,1,1024]{2,1,0:T(1,128)} reshape(f32[2048,2,2,16]{3,2,1,0:T(2,128)} %fusion.923) | data formatting | bytes 1048576
  25.3 10.8 %all-to-all-start = ((f32[128,1,1024]{2,1,0:T(1,128)}), f32[128,1,1024]{2,1,0:T(1,128)S(1)}, u32[]{:S(2)}, u32[]{:S(2)}) async-start(f32[128,1,1024]{2,1,0:T(1,128)} %reshape.1070), calls=%async_computation | async-start | bytes 1048576 | tf_op jit(solution)/shard_map/all_to_all | solution.py:114
  36.1 12.8 %all-to-all-done = f32[128,1,1024]{2,1,0:T(1,128)S(1)} async-done(((f32[128,1,1024]{2,1,0:T(1,128)}), f32[128,1,1024]{2,1,0:T(1,128)S(1)}, u32[]{:S(2)}, u32[]{:S(2)}) %all-to-all-start) | async-done | bytes 524320 | tf_op jit(solution)/shard_map/all_to_all | solution.py:114
  51.5 6.9 %reshape.1071 = f32[2048,2,2,16]{3,2,1,0:T(2,128)} reshape(f32[128,1024]{1,0:T(8,128)S(1)} %reduce) | data formatting | bytes 1048576
  58.5 6.6 %copy.542 = f32[2,2,16,128,16]{2,3,4,1,0:T(8,128)} copy(f32[2,2,16,128,16]{2,1,0,4,3:T(2,128)} %bitcast.781) | data formatting | bytes 1048576 | tf_op jit(solution)/shard_map/all_to_all | solution.py:114
  65.1 4.9 all_to_all.107
  84.8 16.8 %copy.276 = f32[7,1,16,2048]{2,1,0,3:T(1,128)} copy(f32[7,1,16,2048]{3,2,0,1:T(8,128)} %mul.3195) | data formatting | bytes 1835008 | tf_op jit(solution)/shard_map/mul | solution.py:92
  103.9 12.4 %copy.277 = f32[7,1,16,2048]{2,1,0,3:T(1,128)} copy(f32[7,1,16,2048]{3,2,0,1:T(8,128)S(1)} %mul.3198) | data formatting | bytes 1835008 | tf_op jit(solution)/shard_map/mul | solution.py:95
  116.3 19.0 %fusion.921 = f32[2048,7,2,16]{3,2,1,0:T(2,128)} fusion(f32[7,1,16,2048]{2,1,0,3:T(1,128)} %copy.277, f32[7,1,16,2048]{2,1,0,3:T(1,128)} %copy.276), kind=kLoop, calls=%fused_computation.1019 | loop fusion | flops 458752 | bytes 3670016
  135.4 22.7 %reshape.1072 = f32[128,1,3584]{2,1,0:T(1,128)} reshape(f32[2048,7,2,16]{3,2,1,0:T(2,128)} %fusion.921) | data formatting | bytes 3670016
  158.1 31.8 %all_to_all.144 = f32[128,1,3584]{2,1,0:T(1,128)S(1)} all-to-all(f32[128,1,3584]{2,1,0:T(1,128)} %reshape.1072), channel_id=1, replica_groups=mesh['gx'=16,'gz'=8] {'gx','gz'}, dimensions={0} | all-to-all | bytes 3670016 | tf_op jit(solution)/shard_map/all_to_all | solution.py:118
  189.9 6.7 %reduce.1 = f32[128,3584]{1,0:T(8,128)} reduce(f32[128,1,3584]{2,1,0:T(1,128)S(1)} %all_to_all.144, f32[]{:T(128)} %broadcast.1810), dimensions={1}, to_apply=%all_to_all.108.reduce_sub_computation | reduce | bytes 3670020 | tf_op jit(solution)/shard_map/all_to_all | solution.py:118
  196.6 22.7 %reshape.1073 = f32[2048,7,2,16]{3,2,1,0:T(2,128)} reshape(f32[128,3584]{1,0:T(8,128)} %reduce.1) | data formatting | bytes 3670016
  219.3 18.8 %copy.540 = f32[7,2,128,16,16]{4,2,3,1,0:T(8,128)} copy(f32[7,2,128,16,16]{4,1,0,3,2:T(2,128)} %bitcast.779) | data formatting | bytes 3670016 | tf_op jit(solution)/shard_map/all_to_all | solution.py:118
  238.1 13.0 %all_to_all.111 = f32[7,2,16,2048]{3,2,1,0:T(8,128)S(1)} reshape(f32[7,2,16,128,16]{4,3,2,1,0:T(8,128)} %bitcast.780) | data formatting | bytes 3670016 | tf_op jit(solution)/shard_map/all_to_all | solution.py:118
  266.5 5.2 all-to-all-start.2
  283.4 4.1 reshape.1075
  287.5 4.1 copy.547
  306.3 7.4 %fusion.922 = f32[2048,2,2,16]{3,2,1,0:T(2,128)} fusion(f32[2,1,16,2048]{2,1,0,3:T(1,128)} %bitcast.801, f32[2,1,16,2048]{2,1,0,3:T(1,128)} %bitcast.799), kind=kLoop, calls=%fused_computation.1020 | loop fusion | flops 131072 | bytes 1048576
  313.7 8.0 %reshape.1076 = f32[128,1,1024]{2,1,0:T(1,128)} reshape(f32[2048,2,2,16]{3,2,1,0:T(2,128)} %fusion.922) | data formatting | bytes 1048576
  321.6 6.1 %all-to-all-start.3 = ((f32[128,1,1024]{2,1,0:T(1,128)}), f32[128,1,1024]{2,1,0:T(1,128)S(1)}, u32[]{:S(2)}, u32[]{:S(2)}) async-start(f32[128,1,1024]{2,1,0:T(1,128)} %reshape.1076), calls=%async_computation.3 | async-start | bytes 1048576 | tf_op jit(solution)/shard_map/all_to_all | solution.py:118
  330.0 10.7 %all-to-all-done.3 = f32[128,1,1024]{2,1,0:T(1,128)S(1)} async-done(((f32[128,1,1024]{2,1,0:T(1,128)}), f32[128,1,1024]{2,1,0:T(1,128)S(1)}, u32[]{:S(2)}, u32[]{:S(2)}) %all-to-all-start.3) | async-done | bytes 524320 | tf_op jit(solution)/shard_map/all_to_all | solution.py:118
  342.7 6.9 %reshape.1077 = f32[2048,2,2,16]{3,2,1,0:T(2,128)} reshape(f32[128,1024]{1,0:T(8,128)S(1)} %reduce.3) | data formatting | bytes 1048576
  349.6 6.6 %copy.541 = f32[2,2,128,16,16]{4,2,3,1,0:T(8,128)} copy(f32[2,2,128,16,16]{4,1,0,3,2:T(2,128)} %bitcast.783) | data formatting | bytes 1048576 | tf_op jit(solution)/shard_map/all_to_all | solution.py:118
  356.2 5.2 all_to_all.119
  370.9 5.0 reshape.1078
  375.9 5.0 all-to-all-start.4
  382.1 9.2 %all-to-all-done.4 = f32[128,1,512]{2,1,0:T(1,128)S(1)} async-done(((f32[128,1,512]{2,1,0:T(1,128)}), f32[128,1,512]{2,1,0:T(1,128)S(1)}, u32[]{:S(2)}, u32[]{:S(2)}) %all-to-all-start.4) | async-done | bytes 262176 | tf_op jit(solution)/shard_map/all_to_all | solution.py:114
  392.6 4.1 reshape.1079
  396.8 4.1 copy.546
  415.9 5.4 reshape.1080
  421.3 5.8 all-to-all-start.5
  430.7 5.3 collective-permute-start.2
  440.3 4.1 reshape.1081
  444.5 4.1 copy.545
  460.5 5.0 reshape.1082
  465.5 11.2 %all-to-all-start.6 = ((f32[128,1,512]{2,1,0:T(1,128)}), f32[128,1,512]{2,1,0:T(1,128)}, u32[]{:S(2)}, u32[]{:S(2)}) async-start(f32[128,1,512]{2,1,0:T(1,128)} %reshape.1082), calls=%async_computation.6 | async-start | bytes 524288 | tf_op jit(solution)/shard_map/all_to_all | solution.py:114
  477.8 9.0 %all-to-all-done.6 = f32[128,1,512]{2,1,0:T(1,128)} async-done(((f32[128,1,512]{2,1,0:T(1,128)}), f32[128,1,512]{2,1,0:T(1,128)}, u32[]{:S(2)}, u32[]{:S(2)}) %all-to-all-start.6) | async-done | bytes 262176 | tf_op jit(solution)/shard_map/all_to_all | solution.py:114
  489.7 5.1 reshape.1083
  494.8 4.1 copy.544
  518.7 5.2 reshape.1084
  523.9 5.8 all-to-all-start.7
  532.7 7.1 %all-to-all-done.7 = f32[128,1,512]{2,1,0:T(1,128)} async-done(((f32[128,1,512]{2,1,0:T(1,128)}), f32[128,1,512]{2,1,0:T(1,128)}, u32[]{:S(2)}, u32[]{:S(2)}) %all-to-all-start.7) | async-done | bytes 262176 | tf_op jit(solution)/shard_map/all_to_all | solution.py:118
  542.1 4.1 reshape.1085
  546.3 4.1 copy.543
  556.5 33.7 %all_gather.3 = f32[3,128,256]{2,1,0:T(8,128)S(1)} all-gather(f32[3,16,256]{2,1,0:T(8,128)S(1)} %pad_maximum_fusion.14), channel_id=1, replica_groups=mesh['gx'=16,'gz'=8] {'gz'}, dimensions={1}, use_global_device_ids=true | all-gather | bytes 442368 | tf_op jit(solution)/shard_map/all_gather | solution.py:225
  599.4 4.2 collective-permute-done.5
  (284 shorter events, 167.1 us)
Async XLA Ops:
  25.3 23.7 %all-to-all-start = ((f32[128,1,1024]{2,1,0:T(1,128)}), f32[128,1,1024]{2,1,0:T(1,128)S(1)}, u32[]{:S(2)}, u32[]{:S(2)}) async-start(f32[128,1,1024]{2,1,0:T(1,128)} %reshape.1070), calls=%async_computation | async-start | bytes 1048576 | tf_op jit(solution)/shard_map/all_to_all | solution.py:114
  257.0 1.8 copy-start.2
  258.8 106.8 %copy-start.3 = (f32[1,16,16,128]{3,2,1,0:T(8,128)}, f32[1,16,16,128]{3,2,1,0:T(8,128)S(1)}, u32[]{:S(2)}) copy-start(f32[1,16,16,128]{3,2,1,0:T(8,128)S(1)} %get-tuple-element.32) | copy-start | bytes 393220
  266.5 15.6 %all-to-all-start.2 = ((f32[128,1,512]{2,1,0:T(1,128)}), f32[128,1,512]{2,1,0:T(1,128)S(1)}, u32[]{:S(2)}, u32[]{:S(2)}) async-start(f32[128,1,512]{2,1,0:T(1,128)} %reshape.1074), calls=%async_computation.2 | async-start | bytes 524288 | tf_op jit(solution)/shard_map/all_to_all | solution.py:114
  272.4 154.8 %collective-permute-start = (f32[1,8,256]{2,0,1:T(1,128)S(1)}, f32[1,8,256]{2,0,1:T(1,128)S(1)}, u32[]{:S(2)}, u32[]{:S(2)}) collective-permute-start(f32[1,8,256]{2,0,1:T(1,128)S(1)} %copy.322), channel_id=1, source_target_pairs={{8,0},{16,8},{24,16},{32,24},{40,32},{48,40},{56,48},{64,56},{72,6... | collective-permute-start | bytes 24584 | tf_op jit(solution)/shard_map/ppermute | solution.py:23
  276.0 151.2 %collective-permute-start.1 = (f32[1,8,256]{2,0,1:T(1,128)S(1)}, f32[1,8,256]{2,0,1:T(1,128)S(1)}, u32[]{:S(2)}, u32[]{:S(2)}) collective-permute-start(f32[1,8,256]{2,0,1:T(1,128)S(1)} %copy.324), channel_id=1, source_target_pairs={{0,8},{8,16},{16,24},{24,32},{32,40},{40,48},{48,56},{56,64},{64,7... | collective-permute-start | bytes 24584 | tf_op jit(solution)/shard_map/ppermute | solution.py:22
  321.6 19.1 %all-to-all-start.3 = ((f32[128,1,1024]{2,1,0:T(1,128)}), f32[128,1,1024]{2,1,0:T(1,128)S(1)}, u32[]{:S(2)}, u32[]{:S(2)}) async-start(f32[128,1,1024]{2,1,0:T(1,128)} %reshape.1076), calls=%async_computation.3 | async-start | bytes 1048576 | tf_op jit(solution)/shard_map/all_to_all | solution.py:118
  365.5 3.1 copy-start.5
  375.9 15.4 %all-to-all-start.4 = ((f32[128,1,512]{2,1,0:T(1,128)}), f32[128,1,512]{2,1,0:T(1,128)S(1)}, u32[]{:S(2)}, u32[]{:S(2)}) async-start(f32[128,1,512]{2,1,0:T(1,128)} %reshape.1078), calls=%async_computation.4 | async-start | bytes 524288 | tf_op jit(solution)/shard_map/all_to_all | solution.py:114
  415.9 11.2 %copy-start = (f32[128,8,256]{2,1,0:T(8,128)S(1)}, f32[128,8,256]{2,1,0:T(8,128)}, u32[]{:S(2)}) copy-start(f32[128,8,256]{2,1,0:T(8,128)} %param.7) | copy-start | bytes 3145732
  421.3 16.7 %all-to-all-start.5 = ((f32[128,1,512]{2,1,0:T(1,128)}), f32[128,1,512]{2,1,0:T(1,128)}, u32[]{:S(2)}, u32[]{:S(2)}) async-start(f32[128,1,512]{2,1,0:T(1,128)} %reshape.1080), calls=%async_computation.5 | async-start | bytes 524288 | tf_op jit(solution)/shard_map/all_to_all | solution.py:118
  430.7 99.0 %collective-permute-start.2 = (f32[128,1,256]{2,0,1:T(8,128)}, f32[128,1,256]{2,0,1:T(8,128)}, u32[]{:S(2)}, u32[]{:S(2)}) collective-permute-start(f32[128,1,256]{2,0,1:T(8,128)} %get-tuple-element.20), channel_id=1, source_target_pairs={{1,0},{2,1},{3,2},{4,3},{5,4},{6,5},{7,6},{9,8},{10,9},{11,10},{12... | collective-permute-start | bytes 393224 | tf_op jit(solution)/shard_map/ppermute | solution.py:23
  436.0 93.7 %collective-permute-start.3 = (f32[128,1,256]{2,0,1:T(8,128)}, f32[128,1,256]{2,0,1:T(8,128)}, u32[]{:S(2)}, u32[]{:S(2)}) collective-permute-start(f32[128,1,256]{2,0,1:T(8,128)} %get-tuple-element.21), channel_id=1, source_target_pairs={{0,1},{1,2},{2,3},{3,4},{4,5},{5,6},{6,7},{8,9},{9,10},{10,11},{11... | collective-permute-start | bytes 393224 | tf_op jit(solution)/shard_map/ppermute | solution.py:22
  451.7 2.9 copy-start.4
  451.7 2.9 copy-start.6
  451.7 2.9 copy-start.8
  451.7 2.9 copy-start.9
  451.8 2.9 copy-start.10
  451.8 2.9 copy-start.11
  455.0 0.7 copy-start.7
  465.5 21.3 %all-to-all-start.6 = ((f32[128,1,512]{2,1,0:T(1,128)}), f32[128,1,512]{2,1,0:T(1,128)}, u32[]{:S(2)}, u32[]{:S(2)}) async-start(f32[128,1,512]{2,1,0:T(1,128)} %reshape.1082), calls=%async_computation.6 | async-start | bytes 524288 | tf_op jit(solution)/shard_map/all_to_all | solution.py:114
  523.9 16.0 %all-to-all-start.7 = ((f32[128,1,512]{2,1,0:T(1,128)}), f32[128,1,512]{2,1,0:T(1,128)}, u32[]{:S(2)}, u32[]{:S(2)}) async-start(f32[128,1,512]{2,1,0:T(1,128)} %reshape.1084), calls=%async_computation.7 | async-start | bytes 524288 | tf_op jit(solution)/shard_map/all_to_all | solution.py:118
  553.6 2.9 copy-start.13
  553.6 2.9 copy-start.14
  553.6 36.6 %copy-start.1 = (f32[128,7,256]{2,0,1:T(8,128)S(1)}, f32[128,7,256]{2,0,1:T(8,128)}, u32[]{:S(2)}) copy-start(f32[128,7,256]{2,0,1:T(8,128)} %get-tuple-element.17) | copy-start | bytes 2752516
  553.6 36.6 %copy-start.12 = (f32[128,1,256]{2,0,1:T(8,128)S(1)}, f32[128,1,256]{2,0,1:T(8,128)}, u32[]{:S(2)}) copy-start(f32[128,1,256]{2,0,1:T(8,128)} %get-tuple-element.19) | copy-start | bytes 393220
  553.6 36.6 %copy-start.15 = (f32[8]{0:T(128)S(1)}, f32[8]{0:T(128)}, u32[]{:S(2)}) copy-start(f32[8]{0:T(128)} %multiply_subtract_fusion.18) | copy-start | bytes 100
  591.0 8.4 %collective-permute-start.4 = (f32[128,1,256]{2,0,1:T(8,128)S(1)}, f32[128,1,256]{2,0,1:T(8,128)S(1)}, u32[]{:S(2)}, u32[]{:S(2)}) collective-permute-start(f32[128,1,256]{2,0,1:T(8,128)S(1)} %get-tuple-element.14), channel_id=1, source_target_pairs={{1,0},{2,1},{3,2},{4,3},{5,4},{6,5},{7,6},{9,8},{10,9},{11,10},{12... | collective-permute-start | bytes 393224 | tf_op jit(solution)/shard_map/ppermute | solution.py:23
  594.2 9.3 %collective-permute-start.5 = (f32[128,1,256]{2,0,1:T(8,128)S(1)}, f32[128,1,256]{2,0,1:T(8,128)S(1)}, u32[]{:S(2)}, u32[]{:S(2)}) collective-permute-start(f32[128,1,256]{2,0,1:T(8,128)S(1)} %get-tuple-element.15), channel_id=1, source_target_pairs={{0,1},{1,2},{2,3},{3,4},{4,5},{5,6},{6,7},{8,9},{9,10},{10,11},{11... | collective-permute-start | bytes 393224 | tf_op jit(solution)/shard_map/ppermute | solution.py:22
where the time goes:
time: 617 us; the launch traced here: 606 us
  local copies, waits for them, and re-layouts  285 us (46%)
  starting transfers between devices  68.5 us (11%)
  blocking collectives  65.5 us (11%)
  matrix products  63.7 us (10%)
  other arithmetic  63 us (10%)
  waiting for transfers between devices  57.8 us (9%)
    unnamed x80, local copies, waits for them, and re-layouts  133 us
    all_to_all x8, local copies, waits for them, and re-layouts, to_rows(): lax.all_to_all(stacked, ('gx', 'gz'), split_axis=2, concat_axis=3, tiled=...  58.2 us
    all_to_all x4, waiting for transfers between devices, to_columns(): lax.all_to_all(stacked, ('gx', 'gz'), split_axis=3, concat_axis=2, tiled=...  34.8 us
    all_to_all x9, local copies, waits for them, and re-layouts, to_columns(): lax.all_to_all(stacked, ('gx', 'gz'), split_axis=3, concat_axis=2, tiled=...  34.7 us
    unnamed x15, other arithmetic  34.3 us
    all_gather x1, blocking collectives, shards(): surface = lax.all_gather(window, 'gz', axis=1, tiled=True)  33.7 us
    all_to_all x4, starting transfers between devices, to_columns(): lax.all_to_all(stacked, ('gx', 'gz'), split_axis=3, concat_axis=2, tiled=...  32.1 us
    all_to_all x1, blocking collectives, to_rows(): lax.all_to_all(stacked, ('gx', 'gz'), split_axis=2, concat_axis=3, tiled=...  31.8 us
  transfers between devices with their start and end apart: 13, of which 8 were waited for; matrix products, arithmetic and copies ran while one was open for 27% of the time, Pallas kernels for 0%

commit v1 on v0

--- a/solution.py
+++ b/solution.py
@@ -222,7 +222,9 @@
     slope_list = fields_from([derived(real_part[0], imaginary[0], along_x)])
     new_slope = slope_list[0]
     window = jnp.stack([elevation[:, :columns], new_elevation[:, :columns], new_slope[:, :columns]])
-    surface = lax.all_gather(window, "gz", axis=1, tiled=True)
+    surface = jnp.concatenate(
+        lax.all_to_all(jnp.stack([window] * lax.axis_size("gz")), "gz", 0, 0), axis=1
+    )
     old_rows = surface[0]
     new_rows = surface[1]
     slope_rows = surface[2]

time: 617 us -> 579 us (0.938)
  blocking collectives: 65.5 us -> 47.4 us
  local copies, waits for them, and re-layouts: 285 us -> 276 us
  starting transfers between devices: 68.5 us -> 60.3 us
    all_gather x1 -> x0, blocking collectives: 33.7 us -> none  [shards(): surface = lax.all_gather(window, 'gz', axis=1, tiled=True)]
    all_to_all x0 -> x1, blocking collectives: none -> 15.6 us  [to_columns(): lax.all_to_all(stacked, ('gx', 'gz'), split_axis=3, concat_axis=2, tiled=...]
    all_to_all x4 -> x3, starting transfers between devices: 32.1 us -> 20.3 us  [to_columns(): lax.all_to_all(stacked, ('gx', 'gz'), split_axis=3, concat_axis=2, tiled=...]
    all_to_all x0 -> x1, starting transfers between devices: none -> 7.12 us  [shards(): lax.all_to_all(jnp.stack([window] * lax.axis_size('gz')), 'gz', 0, 0)]
    all_to_all x4 -> x3, waiting for transfers between devices: 34.8 us -> 30.5 us  [to_columns(): lax.all_to_all(stacked, ('gx', 'gz'), split_axis=3, concat_axis=2, tiled=...]
    unnamed x80 -> x62, local copies, waits for them, and re-layouts: 133 us -> 130 us
  transfers between devices with their start and end apart: 13 -> 13, of which waited for: 8 -> 9; matrix products, arithmetic and copies ran while one was open for 27% -> 19% of each run, Pallas kernels for 0% -> 0%
where the time goes in v1:
time: 579 us; the launch traced here: 568 us
  local copies, waits for them, and re-layouts  276 us (48%)
  matrix products  63.1 us (11%)
  other arithmetic  60.3 us (10%)
  starting transfers between devices  60.3 us (10%)
  waiting for transfers between devices  58.4 us (10%)
  blocking collectives  47.4 us (8%)
    unnamed x62, local copies, waits for them, and re-layouts  130 us
    all_to_all x8, local copies, waits for them, and re-layouts, to_rows(): lax.all_to_all(stacked, ('gx', 'gz'), split_axis=2, concat_axis=3, tiled=...  57.7 us
    unnamed x15, other arithmetic  34 us
    all_to_all x9, local copies, waits for them, and re-layouts, to_columns(): lax.all_to_all(stacked, ('gx', 'gz'), split_axis=3, concat_axis=2, tiled=...  32.4 us
    all_to_all x1, blocking collectives, to_rows(): lax.all_to_all(stacked, ('gx', 'gz'), split_axis=2, concat_axis=3, tiled=...  31.8 us
    all_to_all x3, waiting for transfers between devices, to_columns(): lax.all_to_all(stacked, ('gx', 'gz'), split_axis=3, concat_axis=2, tiled=...  30.5 us
    all_to_all x3, starting transfers between devices, to_columns(): lax.all_to_all(stacked, ('gx', 'gz'), split_axis=3, concat_axis=2, tiled=...  20.3 us
    mul x5, local copies, waits for them, and re-layouts, transform_last(): real_part = real_part.reshape(leading + (length,)) * factor  20 us
  transfers between devices with their start and end apart: 13, of which 9 were waited for; matrix products, arithmetic and copies ran while one was open for 19% of the time, Pallas kernels for 0%

profile of v1, /device:TPU:8, one launch (start us, length us, event | category | flops | bytes accessed | tf_op | source)
XLA Modules:
  0.0 568.3 jit_solution(14943685306775528808)
XLA Ops:
  8.7 7.0 %fusion.923 = f32[2048,2,2,16]{3,2,1,0:T(2,128)} fusion(f32[2,1,16,2048]{2,1,0,3:T(1,128)} %bitcast.797, f32[2,1,16,2048]{2,1,0,3:T(1,128)S(1)} %bitcast.795), kind=kLoop, calls=%fused_computation.1021 | loop fusion | flops 131072 | bytes 1048576
  15.8 8.0 %reshape.1083 = f32[128,1,1024]{2,1,0:T(1,128)} reshape(f32[2048,2,2,16]{3,2,1,0:T(2,128)} %fusion.923) | data formatting | bytes 1048576
  23.7 10.8 %all-to-all-start = ((f32[128,1,1024]{2,1,0:T(1,128)}), f32[128,1,1024]{2,1,0:T(1,128)S(1)}, u32[]{:S(2)}, u32[]{:S(2)}) async-start(f32[128,1,1024]{2,1,0:T(1,128)} %reshape.1083), calls=%async_computation | async-start | bytes 1048576 | tf_op jit(solution)/shard_map/all_to_all | solution.py:114
  34.6 12.8 %all-to-all-done = f32[128,1,1024]{2,1,0:T(1,128)S(1)} async-done(((f32[128,1,1024]{2,1,0:T(1,128)}), f32[128,1,1024]{2,1,0:T(1,128)S(1)}, u32[]{:S(2)}, u32[]{:S(2)}) %all-to-all-start) | async-done | bytes 524320 | tf_op jit(solution)/shard_map/all_to_all | solution.py:114
  50.0 6.9 %reshape.1084 = f32[2048,2,2,16]{3,2,1,0:T(2,128)} reshape(f32[128,1024]{1,0:T(8,128)S(1)} %reduce) | data formatting | bytes 1048576
  56.9 6.6 %copy.542 = f32[2,2,16,128,16]{2,3,4,1,0:T(8,128)} copy(f32[2,2,16,128,16]{2,1,0,4,3:T(2,128)} %bitcast.778) | data formatting | bytes 1048576 | tf_op jit(solution)/shard_map/all_to_all | solution.py:114
  63.5 4.9 all_to_all.110
  83.3 16.8 %copy.276 = f32[7,1,16,2048]{2,1,0,3:T(1,128)} copy(f32[7,1,16,2048]{3,2,0,1:T(8,128)} %mul.3195) | data formatting | bytes 1835008 | tf_op jit(solution)/shard_map/mul | solution.py:92
  102.4 12.5 %copy.277 = f32[7,1,16,2048]{2,1,0,3:T(1,128)} copy(f32[7,1,16,2048]{3,2,0,1:T(8,128)S(1)} %mul.3198) | data formatting | bytes 1835008 | tf_op jit(solution)/shard_map/mul | solution.py:95
  114.9 19.1 %fusion.921 = f32[2048,7,2,16]{3,2,1,0:T(2,128)} fusion(f32[7,1,16,2048]{2,1,0,3:T(1,128)} %copy.277, f32[7,1,16,2048]{2,1,0,3:T(1,128)} %copy.276), kind=kLoop, calls=%fused_computation.1019 | loop fusion | flops 458752 | bytes 3670016
  134.0 22.7 %reshape.1085 = f32[128,1,3584]{2,1,0:T(1,128)} reshape(f32[2048,7,2,16]{3,2,1,0:T(2,128)} %fusion.921) | data formatting | bytes 3670016
  156.7 31.8 %all_to_all.149 = f32[128,1,3584]{2,1,0:T(1,128)S(1)} all-to-all(f32[128,1,3584]{2,1,0:T(1,128)} %reshape.1085), channel_id=1, replica_groups=mesh['gx'=16,'gz'=8] {'gx','gz'}, dimensions={0} | all-to-all | bytes 3670016 | tf_op jit(solution)/shard_map/all_to_all | solution.py:118
  188.5 6.7 %reduce.1 = f32[128,3584]{1,0:T(8,128)} reduce(f32[128,1,3584]{2,1,0:T(1,128)S(1)} %all_to_all.149, f32[]{:T(128)} %broadcast.1810), dimensions={1}, to_apply=%all_to_all.111.reduce_sub_computation | reduce | bytes 3670020 | tf_op jit(solution)/shard_map/all_to_all | solution.py:118
  195.2 22.7 %reshape.1086 = f32[2048,7,2,16]{3,2,1,0:T(2,128)} reshape(f32[128,3584]{1,0:T(8,128)} %reduce.1) | data formatting | bytes 3670016
  217.9 18.8 %copy.540 = f32[7,2,128,16,16]{4,2,3,1,0:T(8,128)} copy(f32[7,2,128,16,16]{4,1,0,3,2:T(2,128)} %bitcast.776) | data formatting | bytes 3670016 | tf_op jit(solution)/shard_map/all_to_all | solution.py:118
  236.7 13.0 %all_to_all.114 = f32[7,2,16,2048]{3,2,1,0:T(8,128)S(1)} reshape(f32[7,2,16,128,16]{4,3,2,1,0:T(8,128)} %bitcast.777) | data formatting | bytes 3670016 | tf_op jit(solution)/shard_map/all_to_all | solution.py:118
  264.3 15.6 %all_to_all.150 = f32[128,1,512]{2,1,0:T(1,128)S(1)} all-to-all(f32[128,1,512]{2,1,0:T(1,128)S(1)} %reshape.1087), channel_id=1, replica_groups=mesh['gx'=16,'gz'=8] {'gx','gz'}, dimensions={0} | all-to-all | bytes 524288 | tf_op jit(solution)/shard_map/all_to_all | solution.py:114
  303.5 7.0 %fusion.922 = f32[2048,2,2,16]{3,2,1,0:T(2,128)} fusion(f32[2,1,16,2048]{2,1,0,3:T(1,128)} %bitcast.798, f32[2,1,16,2048]{2,1,0,3:T(1,128)S(1)} %bitcast.796), kind=kLoop, calls=%fused_computation.1020 | loop fusion | flops 131072 | bytes 1048576
  310.5 8.0 %reshape.1089 = f32[128,1,1024]{2,1,0:T(1,128)} reshape(f32[2048,2,2,16]{3,2,1,0:T(2,128)} %fusion.922) | data formatting | bytes 1048576
  318.5 4.9 all-to-all-start.3
  331.1 5.5 all-to-all-done.3
  338.5 7.3 %reshape.1090 = f32[2048,2,2,16]{3,2,1,0:T(2,128)} reshape(f32[128,1024]{1,0:T(8,128)S(1)} %reduce.3) | data formatting | bytes 1048576
  345.8 6.6 %copy.541 = f32[2,2,128,16,16]{4,2,3,1,0:T(8,128)} copy(f32[2,2,128,16,16]{4,1,0,3,2:T(2,128)} %bitcast.780) | data formatting | bytes 1048576 | tf_op jit(solution)/shard_map/all_to_all | solution.py:118
  352.4 4.7 all_to_all.122
  366.0 5.2 reshape.1091
  371.1 4.7 all-to-all-start.4
  376.4 10.0 %all-to-all-done.4 = f32[128,1,512]{2,1,0:T(1,128)S(1)} async-done(((f32[128,1,512]{2,1,0:T(1,128)}), f32[128,1,512]{2,1,0:T(1,128)S(1)}, u32[]{:S(2)}, u32[]{:S(2)}) %all-to-all-start.4) | async-done | bytes 262176 | tf_op jit(solution)/shard_map/all_to_all | solution.py:114
  387.7 4.1 reshape.1092
  391.8 4.1 copy.546
  411.0 5.4 reshape.1093
  416.4 4.8 all-to-all-start.5
  422.3 9.3 %all-to-all-done.5 = f32[128,1,512]{2,1,0:T(1,128)S(1)} async-done(((f32[128,1,512]{2,1,0:T(1,128)}), f32[128,1,512]{2,1,0:T(1,128)S(1)}, u32[]{:S(2)}, u32[]{:S(2)}) %all-to-all-start.5) | async-done | bytes 262176 | tf_op jit(solution)/shard_map/all_to_all | solution.py:118
  433.0 4.1 reshape.1094
  437.1 4.1 copy.545
  452.9 5.1 reshape.1095
  458.0 4.8 all-to-all-start.6
  465.6 7.7 %all-to-all-done.6 = f32[128,1,512]{2,1,0:T(1,128)S(1)} async-done(((f32[128,1,512]{2,1,0:T(1,128)}), f32[128,1,512]{2,1,0:T(1,128)S(1)}, u32[]{:S(2)}, u32[]{:S(2)}) %all-to-all-start.6) | async-done | bytes 262176 | tf_op jit(solution)/shard_map/all_to_all | solution.py:114
  474.7 4.1 reshape.1096
  478.8 4.1 copy.544
  497.9 5.2 reshape.1097
  503.1 4.8 all-to-all-start.7
  508.7 5.3 collective-permute-start.2
  519.9 4.1 reshape.1098
  524.1 4.1 copy.543
  535.0 7.1 %all-to-all-start.8 = ((f32[8,3,16,256]{3,2,1,0:T(8,128)}), f32[8,3,16,256]{3,2,1,0:T(8,128)S(1)}, u32[]{:S(2)}, u32[]{:S(2)}) async-start(f32[8,3,16,256]{3,2,1,0:T(8,128)} %stack.113), calls=%async_computation.8 | async-start | bytes 786432 | tf_op jit(solution)/shard_map/all_to_all | solution.py:226
  544.9 4.9 all-to-all-done.8
  551.8 4.4 collective-permute-start.4
  560.2 5.3 collective-permute-done.5
  (267 shorter events, 157.7 us)
Async XLA Ops:
  23.7 23.7 %all-to-all-start = ((f32[128,1,1024]{2,1,0:T(1,128)}), f32[128,1,1024]{2,1,0:T(1,128)S(1)}, u32[]{:S(2)}, u32[]{:S(2)}) async-start(f32[128,1,1024]{2,1,0:T(1,128)} %reshape.1083), calls=%async_computation | async-start | bytes 1048576 | tf_op jit(solution)/shard_map/all_to_all | solution.py:114
  255.6 1.8 copy-start.1
  318.5 18.0 %all-to-all-start.3 = ((f32[128,1,1024]{2,1,0:T(1,128)}), f32[128,1,1024]{2,1,0:T(1,128)S(1)}, u32[]{:S(2)}, u32[]{:S(2)}) async-start(f32[128,1,1024]{2,1,0:T(1,128)} %reshape.1089), calls=%async_computation.3 | async-start | bytes 1048576 | tf_op jit(solution)/shard_map/all_to_all | solution.py:118
  324.1 138.8 %collective-permute-start = (f32[1,8,256]{2,0,1:T(1,128)S(1)}, f32[1,8,256]{2,0,1:T(1,128)S(1)}, u32[]{:S(2)}, u32[]{:S(2)}) collective-permute-start(f32[1,8,256]{2,0,1:T(1,128)S(1)} %copy.322), channel_id=1, source_target_pairs={{8,0},{16,8},{24,16},{32,24},{40,32},{48,40},{56,48},{64,56},{72,6... | collective-permute-start | bytes 24584 | tf_op jit(solution)/shard_map/ppermute | solution.py:23
  327.7 135.1 %collective-permute-start.1 = (f32[1,8,256]{2,0,1:T(1,128)S(1)}, f32[1,8,256]{2,0,1:T(1,128)S(1)}, u32[]{:S(2)}, u32[]{:S(2)}) collective-permute-start(f32[1,8,256]{2,0,1:T(1,128)S(1)} %copy.324), channel_id=1, source_target_pairs={{0,8},{8,16},{16,24},{24,32},{32,40},{40,48},{48,56},{56,64},{64,7... | collective-permute-start | bytes 24584 | tf_op jit(solution)/shard_map/ppermute | solution.py:22
  371.1 15.3 %all-to-all-start.4 = ((f32[128,1,512]{2,1,0:T(1,128)}), f32[128,1,512]{2,1,0:T(1,128)S(1)}, u32[]{:S(2)}, u32[]{:S(2)}) async-start(f32[128,1,512]{2,1,0:T(1,128)} %reshape.1091), calls=%async_computation.4 | async-start | bytes 524288 | tf_op jit(solution)/shard_map/all_to_all | solution.py:114
  416.4 15.3 %all-to-all-start.5 = ((f32[128,1,512]{2,1,0:T(1,128)}), f32[128,1,512]{2,1,0:T(1,128)S(1)}, u32[]{:S(2)}, u32[]{:S(2)}) async-start(f32[128,1,512]{2,1,0:T(1,128)} %reshape.1093), calls=%async_computation.5 | async-start | bytes 524288 | tf_op jit(solution)/shard_map/all_to_all | solution.py:118
  444.4 2.8 copy-start.3
  444.4 2.8 copy-start.4
  444.4 2.8 copy-start.5
  447.6 3.0 copy-start.2
  450.6 12.3 %copy-start = (f32[128,8,256]{2,1,0:T(8,128)S(1)}, f32[128,8,256]{2,1,0:T(8,128)}, u32[]{:S(2)}) copy-start(f32[128,8,256]{2,1,0:T(8,128)} %param.7) | copy-start | bytes 3145732
  458.0 15.3 %all-to-all-start.6 = ((f32[128,1,512]{2,1,0:T(1,128)}), f32[128,1,512]{2,1,0:T(1,128)S(1)}, u32[]{:S(2)}, u32[]{:S(2)}) async-start(f32[128,1,512]{2,1,0:T(1,128)} %reshape.1095), calls=%async_computation.6 | async-start | bytes 524288 | tf_op jit(solution)/shard_map/all_to_all | solution.py:114
  503.1 15.5 %all-to-all-start.7 = ((f32[128,1,512]{2,1,0:T(1,128)}), f32[128,1,512]{2,1,0:T(1,128)S(1)}, u32[]{:S(2)}, u32[]{:S(2)}) async-start(f32[128,1,512]{2,1,0:T(1,128)} %reshape.1097), calls=%async_computation.7 | async-start | bytes 524288 | tf_op jit(solution)/shard_map/all_to_all | solution.py:118
  508.7 34.6 %collective-permute-start.2 = (f32[128,1,256]{2,0,1:T(8,128)}, f32[128,1,256]{2,0,1:T(8,128)S(1)}, u32[]{:S(2)}, u32[]{:S(2)}) collective-permute-start(f32[128,1,256]{2,0,1:T(8,128)} %get-tuple-element.20), channel_id=1, source_target_pairs={{1,0},{2,1},{3,2},{4,3},{5,4},{6,5},{7,6},{9,8},{10,9},{11,10},{12... | collective-permute-start | bytes 393224 | tf_op jit(solution)/shard_map/ppermute | solution.py:23
  514.0 29.2 %collective-permute-start.3 = (f32[128,1,256]{2,0,1:T(8,128)}, f32[128,1,256]{2,0,1:T(8,128)}, u32[]{:S(2)}, u32[]{:S(2)}) collective-permute-start(f32[128,1,256]{2,0,1:T(8,128)} %get-tuple-element.21), channel_id=1, source_target_pairs={{0,1},{1,2},{2,3},{3,4},{4,5},{5,6},{6,7},{8,9},{9,10},{10,11},{11... | collective-permute-start | bytes 393224 | tf_op jit(solution)/shard_map/ppermute | solution.py:22
  535.0 14.8 %all-to-all-start.8 = ((f32[8,3,16,256]{3,2,1,0:T(8,128)}), f32[8,3,16,256]{3,2,1,0:T(8,128)S(1)}, u32[]{:S(2)}, u32[]{:S(2)}) async-start(f32[8,3,16,256]{3,2,1,0:T(8,128)} %stack.113), calls=%async_computation.8 | async-start | bytes 786432 | tf_op jit(solution)/shard_map/all_to_all | solution.py:226
  542.1 7.8 %copy-start.6 = (f32[8]{0:T(128)S(1)}, f32[8]{0:T(128)}, u32[]{:S(2)}) copy-start(f32[8]{0:T(128)} %multiply_subtract_fusion.18) | copy-start | bytes 100
  551.8 8.4 %collective-permute-start.4 = (f32[128,1,256]{2,0,1:T(8,128)S(1)}, f32[128,1,256]{2,0,1:T(8,128)S(1)}, u32[]{:S(2)}, u32[]{:S(2)}) collective-permute-start(f32[128,1,256]{2,0,1:T(8,128)S(1)} %get-tuple-element.14), channel_id=1, source_target_pairs={{1,0},{2,1},{3,2},{4,3},{5,4},{6,5},{7,6},{9,8},{10,9},{11,10},{12... | collective-permute-start | bytes 393224 | tf_op jit(solution)/shard_map/ppermute | solution.py:23
  556.2 9.3 %collective-permute-start.5 = (f32[128,1,256]{2,0,1:T(8,128)S(1)}, f32[128,1,256]{2,0,1:T(8,128)S(1)}, u32[]{:S(2)}, u32[]{:S(2)}) collective-permute-start(f32[128,1,256]{2,0,1:T(8,128)S(1)} %get-tuple-element.15), channel_id=1, source_target_pairs={{0,1},{1,2},{2,3},{3,4},{4,5},{5,6},{6,7},{8,9},{9,10},{10,11},{11... | collective-permute-start | bytes 393224 | tf_op jit(solution)/shard_map/ppermute | solution.py:22
